TPU v7x, 512 devices: a whole 4x8x8 slice. The times are simulated.
512 devices in a mesh: blk: 64 (over y_hi, z, core), event: 8 (over x, y_lo).
Axes of the slice: x: 4, y: 8 (y_hi: 4, y_lo: 2; y = y_hi * 2 + y_lo), z: 8, core: 2. Of those that a mesh axis runs over, the one named last changes fastest.
Arguments:
- adjoint_now: float32 [8, 3, 512, 64, 128], P('event', None, 'blk'), may hold values from -6 to 6
- adjoint_prev: float32 [8, 3, 512, 64, 128], P('event', None, 'blk'), may hold values from -6 to 6
- forward_field: float32 [8, 2, 3, 512, 64, 128], P('event', None, None, 'blk'), may hold values from -6 to 6
- density: float32 [512, 64, 128], P('blk'), may hold values from 0.5 to 2
- lame_first: float32 [512, 64, 128], P('blk'), may hold values from 0.5 to 2
- shear_modulus: float32 [512, 64, 128], P('blk'), may hold values from 0.3 to 1.2
Outputs:
- adjoint_field: float32 [8, 3, 512, 64, 128], P('event', None, 'blk')
- shear_kernel: float32 [512, 64, 128], P('blk', 'event')
- bulk_kernel: float32 [512, 64, 128], P('blk', 'event')
All inputs are finite; a program needn't handle non-finite values.
Results may differ from a plain program's by a relative error of at most 0.00002.
Values sent between devices are 32-bit elements; how exact they have to be, the bound alone decides.
A program may use at most 64 MiB of HBM per device.

v0:
```python
import jax
import jax.numpy as jnp
from jax import lax
from jax.sharding import PartitionSpec as P

time_step = 0.3


def with_halo(block, sides, width):
    for axis, dim in sides:
        count = lax.axis_size(axis)
        forward = [(i, i + 1) for i in range(count - 1)]
        forward.append((count - 1, 0))
        backward = [(target, source) for source, target in forward]
        low = lax.ppermute(
            lax.slice_in_dim(block, block.shape[dim] - width, None, axis=dim), axis, forward
        )
        high = lax.ppermute(lax.slice_in_dim(block, 0, width, axis=dim), axis, backward)
        block = jnp.concatenate([low, block, high], axis=dim)
    return block


def slope_long(values):
    return (values[2:] - values[:-2]) * 0.5


def slope_mid(values, axis):
    padded = jnp.pad(values, [(1, 1) if dimension == axis else (0, 0) for dimension in range(3)])
    upper = lax.slice_in_dim(padded, 2, padded.shape[axis], axis=axis)
    lower = lax.slice_in_dim(padded, 0, padded.shape[axis] - 2, axis=axis)
    return (upper - lower) * 0.5


def gradient(field):
    table = [[None, None, None], [None, None, None], [None, None, None]]
    for second in range(3):
        component = field[second]
        middle = component[1:-1]
        table[0][second] = slope_long(component)
        table[1][second] = slope_mid(middle, 1)
        table[2][second] = slope_mid(middle, 2)
    return table


def strain_of(table):
    strain = [
        [0.5 * (table[first][second] + table[second][first]) for second in range(3)]
        for first in range(3)
    ]
    trace = strain[0][0] + strain[1][1] + strain[2][2]
    return (strain, trace)


def stress_of(strain, trace, first_lame, shear_part):
    stress = []
    for first in range(3):
        stress_row = []
        for second in range(3):
            entry = 2.0 * shear_part * strain[first][second]
            if first == second:
                entry = entry + first_lame * trace
            stress_row.append(entry)
        stress.append(stress_row)
    return stress


def divergence(stress):
    result = []
    for second in range(3):
        total = slope_long(stress[0][second])
        total = total + slope_mid(stress[1][second], 1)[1:-1]
        total = total + slope_mid(stress[2][second], 2)[1:-1]
        result.append(total)
    return result


def crop(values, count, axis):
    return lax.slice_in_dim(values, count, values.shape[axis] - count, axis=axis)


def kernel_terms(strain, trace, forward_strain, forward_trace, first_lame, shear_part):
    contracted = strain[0][0] * forward_strain[0][0]
    for first in range(3):
        for second in range(3):
            if first + second > 0:
                contracted = contracted + strain[first][second] * forward_strain[first][second]
    shear_term = -2.0 * time_step * shear_part * (contracted - trace * forward_trace / 3.0)
    bulk_term = -time_step * (first_lame + 2.0 * shear_part / 3.0) * trace * forward_trace
    return (shear_term, bulk_term)


def advance(wide, prev_cut, model_cut, dens_cut, forward_wide, slab_cells):
    strain, trace = strain_of(gradient(wide))
    stress = stress_of(strain, trace, model_cut[0], model_cut[1])
    accel = jnp.stack(divergence(stress))
    updated = 2.0 * crop(wide, 2, 1) - prev_cut + time_step * time_step * accel / dens_cut
    margin = (wide.shape[1] - slab_cells) // 2
    inner = [[crop(entry, margin - 1, 0) for entry in strain_row] for strain_row in strain]
    inner_trace = crop(trace, margin - 1, 0)
    forward_strain, forward_trace = strain_of(gradient(forward_wide))
    model_margin = (model_cut.shape[1] - slab_cells) // 2
    first_lame = crop(model_cut[0], model_margin, 0)
    shear_part = crop(model_cut[1], model_margin, 0)
    return (
        updated,
        kernel_terms(inner, inner_trace, forward_strain, forward_trace, first_lame, shear_part),
    )


def local(adjoint_now, adjoint_prev, forward_field, density, lame_first, shear_modulus):
    slab_cells = density.shape[0]
    current = adjoint_now[0]
    former = adjoint_prev[0]
    forward = forward_field[0]
    step_count = forward.shape[0]
    forward_wide = with_halo(forward, (("blk", 2),), 1)
    moduli = jnp.stack([lame_first, shear_modulus])
    shear_total = jnp.zeros(density.shape, jnp.float32)
    bulk_total = jnp.zeros(density.shape, jnp.float32)
    band_shear = None
    band_bulk = None
    model_wide = with_halo(moduli, (("blk", 1),), 1)
    for step in range(step_count):
        wide = with_halo(current, (("blk", 1),), 2)
        updated, terms = advance(wide, former, model_wide, density, forward_wide[step], slab_cells)
        shear_total = shear_total + terms[0]
        bulk_total = bulk_total + terms[1]
        former = current
        current = updated
    band_shear, band_bulk = (
        lax.psum_scatter(shear_total, "event", scatter_dimension=1, tiled=True),
        lax.psum_scatter(bulk_total, "event", scatter_dimension=1, tiled=True),
    )
    return (current[None], band_shear, band_bulk)


def solution(mesh):
    in_specs = (
        P("event", None, "blk", None, None),
        P("event", None, "blk", None, None),
        P("event", None, None, "blk", None, None),
        P("blk", None, None),
        P("blk", None, None),
        P("blk", None, None),
    )
    out_specs = (
        P("event", None, "blk", None, None),
        P("blk", "event", None),
        P("blk", "event", None),
    )
    return jax.shard_map(local, mesh=mesh, in_specs=in_specs, out_specs=out_specs, check_vma=False)
```

profile of v0, /device:TPU:16, one launch (start us, length us, event | category | flops | bytes accessed | tf_op | source)
XLA Modules:
  0.0 162.9 jit_solution(2566628150719486172)
XLA Ops:
  7.2 0.9 pad_maximum_fusion.12
  8.1 10.3 %collective-permute-start.1 = (f32[2,1,64,128]{3,2,1,0:T(8,128)S(1)}, f32[2,1,64,128]{3,2,1,0:T(8,128)S(1)}, u32[]{:S(2)}, u32[]{:S(2)}) collective-permute-start(f32[2,1,64,128]{3,2,1,0:T(8,128)S(1)} %get-tuple-element.66), channel_id=1, source_target_pairs={{8,0},{16,8},{24,16},{32,24},{40,32},{48,40},{56,48},{64,56},{72,6... | collective-permute-start | bytes 196616 | tf_op jit(solution)/shard_map/ppermute | solution.py:18
  18.4 1.9 %collective-permute-start = (f32[2,1,64,128]{3,2,1,0:T(8,128)S(1)}, f32[2,1,64,128]{3,2,1,0:T(8,128)S(1)}, u32[]{:S(2)}, u32[]{:S(2)}) collective-permute-start(f32[2,1,64,128]{3,2,1,0:T(8,128)S(1)} %get-tuple-element.65), channel_id=1, source_target_pairs={{0,8},{8,16},{16,24},{24,32},{32,40},{40,48},{48,56},{56,64},{64,7... | collective-permute-start | bytes 196616 | tf_op jit(solution)/shard_map/ppermute | solution.py:15
  20.3 1.1 fusion.197
  21.4 1.9 %collective-permute-start.3 = (f32[3,2,64,128]{3,2,1,0:T(8,128)S(1)}, f32[3,2,64,128]{3,2,1,0:T(8,128)S(1)}, u32[]{:S(2)}, u32[]{:S(2)}) collective-permute-start(f32[3,2,64,128]{3,2,1,0:T(8,128)S(1)} %get-tuple-element.60), channel_id=1, source_target_pairs={{0,8},{8,16},{16,24},{24,32},{32,40},{40,48},{48,56},{56,64},{64,7... | collective-permute-start | bytes 589832 | tf_op jit(solution)/shard_map/ppermute | solution.py:15
  23.3 6.7 %collective-permute-start.2 = (f32[3,2,64,128]{3,2,1,0:T(8,128)S(1)}, f32[3,2,64,128]{3,2,1,0:T(8,128)S(1)}, u32[]{:S(2)}, u32[]{:S(2)}) collective-permute-start(f32[3,2,64,128]{3,2,1,0:T(8,128)S(1)} %get-tuple-element.59), channel_id=1, source_target_pairs={{8,0},{16,8},{24,16},{32,24},{40,32},{48,40},{56,48},{64,56},{72,6... | collective-permute-start | bytes 589832 | tf_op jit(solution)/shard_map/ppermute | solution.py:18
  30.0 1.1 fusion.195
  31.0 1.9 %collective-permute-start.7 = (f32[2,3,1,64,128]{4,3,2,1,0:T(8,128)S(1)}, f32[2,3,1,64,128]{4,3,2,1,0:T(8,128)S(1)}, u32[]{:S(2)}, u32[]{:S(2)}) collective-permute-start(f32[2,3,1,64,128]{4,3,2,1,0:T(8,128)S(1)} %get-tuple-element.36), channel_id=1, source_target_pairs={{0,8},{8,16},{16,24},{24,32},{32,40},{40,48},{48,56},{56,64},{64,7... | collective-permute-start | bytes 589832 | tf_op jit(solution)/shard_map/ppermute | solution.py:15
  33.0 6.7 %collective-permute-start.6 = (f32[2,3,1,64,128]{4,3,2,1,0:T(8,128)S(1)}, f32[2,3,1,64,128]{4,3,2,1,0:T(8,128)S(1)}, u32[]{:S(2)}, u32[]{:S(2)}) collective-permute-start(f32[2,3,1,64,128]{4,3,2,1,0:T(8,128)S(1)} %get-tuple-element.35), channel_id=1, source_target_pairs={{8,0},{16,8},{24,16},{32,24},{40,32},{48,40},{56,48},{64,56},{72,6... | collective-permute-start | bytes 589832 | tf_op jit(solution)/shard_map/ppermute | solution.py:18
  39.9 0.5 fusion.178
  41.0 0.4 pad_slice_fusion.29
  41.9 0.4 copy-done.11
  42.4 0.7 copy-done.7
  43.5 2.1 %collective-permute-start.5 = (f32[3,2,64,128]{3,2,1,0:T(8,128)S(1)}, f32[3,2,64,128]{3,2,1,0:T(8,128)S(1)}, u32[]{:S(2)}, u32[]{:S(2)}) collective-permute-start(f32[3,2,64,128]{3,2,1,0:T(8,128)S(1)} %get-tuple-element.58), channel_id=1, source_target_pairs={{0,8},{8,16},{16,24},{24,32},{32,40},{40,48},{48,56},{56,64},{64,7... | collective-permute-start | bytes 589832 | tf_op jit(solution)/shard_map/ppermute | solution.py:15
  45.5 6.7 %collective-permute-start.4 = (f32[3,2,64,128]{3,2,1,0:T(8,128)S(1)}, f32[3,2,64,128]{3,2,1,0:T(8,128)S(1)}, u32[]{:S(2)}, u32[]{:S(2)}) collective-permute-start(f32[3,2,64,128]{3,2,1,0:T(8,128)S(1)} %get-tuple-element.57), channel_id=1, source_target_pairs={{8,0},{16,8},{24,16},{32,24},{40,32},{48,40},{56,48},{64,56},{72,6... | collective-permute-start | bytes 589832 | tf_op jit(solution)/shard_map/ppermute | solution.py:18
  52.4 1.3 collective-permute-done.5
  53.7 3.8 %collective-permute-done.4 = f32[3,2,64,128]{3,2,1,0:T(8,128)S(1)} collective-permute-done((f32[3,2,64,128]{3,2,1,0:T(8,128)S(1)}, f32[3,2,64,128]{3,2,1,0:T(8,128)S(1)}, u32[]{:S(2)}, u32[]{:S(2)}) %collective-permute-start.4) | collective-permute-done | bytes 196640 | tf_op jit(solution)/shard_map/ppermute | solution.py:18
  57.6 1.3 fusion.175
  58.9 0.4 fusion.177
  59.3 1.1 pad_slice_fusion.17
  60.4 0.9 pad_slice_fusion.57
  61.3 1.1 pad_slice_fusion.23
  62.5 0.6 copy-done.33
  63.1 2.0 %fusion.112 = f32[8,64,128]{2,1,0:T(8,128)} fusion(f32[10,64,128]{2,1,0:T(8,128)S(1)} %get-tuple-element.39, f32[10,64,128]{2,1,0:T(8,128)S(1)} %get-tuple-element.40, f32[8,64,128]{2,1,0:T(8,128)S(1)} %get-tuple-element.31, f32[8,64,128]{2,1,0:T(8,128)S(1)} %get-tuple-element.30, f32[10,64,128]{2,1,0:T(8,128)S(1)} %get-tuple-element.13, ...), kind=kLoop, calls=%fused_computation.228 | loop fusion | flops 6225920 | bytes 7733248 | tf_op jit(solution)/shard_map/add | solution.py:126
  65.3 0.9 pad_slice_fusion.59
  66.2 2.8 %pad_slice_fusion.19 = (f32[10,64,128]{2,1,0:T(8,128)}, f32[10,64,128]{2,1,0:T(8,128)}, f32[10,64,128]{2,1,0:T(8,128)}, f32[10,64,128]{2,1,0:T(8,128)}) fusion(f32[10,64,128]{2,1,0:T(8,128)} %get-tuple-element.12), kind=kLoop, calls=%fused_computation.31 | loop fusion | bytes 1638400 | tf_op jit(solution)/shard_map/slice | solution.py:29
  69.0 1.1 multiply_add_fusion.4
  70.2 1.4 fusion.144
  71.7 1.3 fusion.150
  73.4 1.2 fusion.4
  74.6 37.2 %reduce-scatter.3.cloned.1.call-done = f32[8,8,128]{2,1,0:T(8,128)} async-done(((f32[8,64,128]{2,1,0:T(8,128)}), f32[8,8,128]{2,1,0:T(8,128)}) %reduce-scatter.3.cloned.1.call-update) | async-done | bytes 32784 | tf_op jit(solution)/shard_map/reduce_scatter | solution.py:131
  111.8 44.3 %reduce-scatter.5.cloned.1.call-done = f32[8,8,128]{2,1,0:T(8,128)} async-done(((f32[8,64,128]{2,1,0:T(8,128)}), f32[8,8,128]{2,1,0:T(8,128)}) %reduce-scatter.5.cloned.1.call-update) | async-done | bytes 32784 | tf_op jit(solution)/shard_map/reduce_scatter | solution.py:132
  (90 shorter events, 2.4 us)
Async XLA Ops:
  7.2 32.5 %copy-start.4 = (f32[8,64,128]{2,1,0:T(8,128)S(1)}, f32[8,64,128]{2,1,0:T(8,128)}, u32[]{:S(2)}) copy-start(f32[8,64,128]{2,1,0:T(8,128)} %param.11) | copy-start | bytes 786436
  7.2 32.5 %copy-start.9 = (f32[8,64,128]{2,1,0:T(8,128)S(1)}, f32[8,64,128]{2,1,0:T(8,128)}, u32[]{:S(2)}) copy-start(f32[8,64,128]{2,1,0:T(8,128)} %param.10) | copy-start | bytes 786436
  7.2 104.7 %reduce-scatter.3.cloned.1.call-start = ((), (), s32[]{:S(2)}) async-start(), calls=%async_computation.2 | async-start | bytes 294912 | tf_op jit(solution)/shard_map/reduce_scatter | solution.py:131
  8.1 31.7 %copy-start = (f32[1,3,8,64,128]{4,3,2,1,0:T(8,128)S(1)}, f32[1,3,8,64,128]{4,3,2,1,0:T(8,128)}, u32[]{:S(2)}) copy-start(f32[1,3,8,64,128]{4,3,2,1,0:T(8,128)} %param.6) | copy-start | bytes 2359300
  8.1 24.9 %collective-permute-start.1 = (f32[2,1,64,128]{3,2,1,0:T(8,128)S(1)}, f32[2,1,64,128]{3,2,1,0:T(8,128)S(1)}, u32[]{:S(2)}, u32[]{:S(2)}) collective-permute-start(f32[2,1,64,128]{3,2,1,0:T(8,128)S(1)} %get-tuple-element.66), channel_id=1, source_target_pairs={{8,0},{16,8},{24,16},{32,24},{40,32},{48,40},{56,48},{64,56},{72,6... | collective-permute-start | bytes 196616 | tf_op jit(solution)/shard_map/ppermute | solution.py:18
  18.4 21.2 %collective-permute-start = (f32[2,1,64,128]{3,2,1,0:T(8,128)S(1)}, f32[2,1,64,128]{3,2,1,0:T(8,128)S(1)}, u32[]{:S(2)}, u32[]{:S(2)}) collective-permute-start(f32[2,1,64,128]{3,2,1,0:T(8,128)S(1)} %get-tuple-element.65), channel_id=1, source_target_pairs={{0,8},{8,16},{16,24},{24,32},{32,40},{40,48},{48,56},{56,64},{64,7... | collective-permute-start | bytes 196616 | tf_op jit(solution)/shard_map/ppermute | solution.py:15
  21.4 18.3 %collective-permute-start.3 = (f32[3,2,64,128]{3,2,1,0:T(8,128)S(1)}, f32[3,2,64,128]{3,2,1,0:T(8,128)S(1)}, u32[]{:S(2)}, u32[]{:S(2)}) collective-permute-start(f32[3,2,64,128]{3,2,1,0:T(8,128)S(1)} %get-tuple-element.60), channel_id=1, source_target_pairs={{0,8},{8,16},{16,24},{24,32},{32,40},{40,48},{48,56},{56,64},{64,7... | collective-permute-start | bytes 589832 | tf_op jit(solution)/shard_map/ppermute | solution.py:15
  23.3 16.4 %collective-permute-start.2 = (f32[3,2,64,128]{3,2,1,0:T(8,128)S(1)}, f32[3,2,64,128]{3,2,1,0:T(8,128)S(1)}, u32[]{:S(2)}, u32[]{:S(2)}) collective-permute-start(f32[3,2,64,128]{3,2,1,0:T(8,128)S(1)} %get-tuple-element.59), channel_id=1, source_target_pairs={{8,0},{16,8},{24,16},{32,24},{40,32},{48,40},{56,48},{64,56},{72,6... | collective-permute-start | bytes 589832 | tf_op jit(solution)/shard_map/ppermute | solution.py:18
  31.0 31.4 %collective-permute-start.7 = (f32[2,3,1,64,128]{4,3,2,1,0:T(8,128)S(1)}, f32[2,3,1,64,128]{4,3,2,1,0:T(8,128)S(1)}, u32[]{:S(2)}, u32[]{:S(2)}) collective-permute-start(f32[2,3,1,64,128]{4,3,2,1,0:T(8,128)S(1)} %get-tuple-element.36), channel_id=1, source_target_pairs={{0,8},{8,16},{16,24},{24,32},{32,40},{40,48},{48,56},{56,64},{64,7... | collective-permute-start | bytes 589832 | tf_op jit(solution)/shard_map/ppermute | solution.py:15
  33.0 29.5 %collective-permute-start.6 = (f32[2,3,1,64,128]{4,3,2,1,0:T(8,128)S(1)}, f32[2,3,1,64,128]{4,3,2,1,0:T(8,128)S(1)}, u32[]{:S(2)}, u32[]{:S(2)}) collective-permute-start(f32[2,3,1,64,128]{4,3,2,1,0:T(8,128)S(1)} %get-tuple-element.35), channel_id=1, source_target_pairs={{8,0},{16,8},{24,16},{32,24},{40,32},{48,40},{56,48},{64,56},{72,6... | collective-permute-start | bytes 589832 | tf_op jit(solution)/shard_map/ppermute | solution.py:18
  43.1 9.1 %copy-start.1 = (f32[1,2,3,8,64,128]{5,4,3,2,1,0:T(8,128)S(1)}, f32[1,2,3,8,64,128]{5,4,3,2,1,0:T(8,128)}, u32[]{:S(2)}) copy-start(f32[1,2,3,8,64,128]{5,4,3,2,1,0:T(8,128)} %param.8) | copy-start | bytes 4718596
  43.5 10.2 %collective-permute-start.5 = (f32[3,2,64,128]{3,2,1,0:T(8,128)S(1)}, f32[3,2,64,128]{3,2,1,0:T(8,128)S(1)}, u32[]{:S(2)}, u32[]{:S(2)}) collective-permute-start(f32[3,2,64,128]{3,2,1,0:T(8,128)S(1)} %get-tuple-element.58), channel_id=1, source_target_pairs={{0,8},{8,16},{16,24},{24,32},{32,40},{40,48},{48,56},{56,64},{64,7... | collective-permute-start | bytes 589832 | tf_op jit(solution)/shard_map/ppermute | solution.py:15
  45.5 11.9 %collective-permute-start.4 = (f32[3,2,64,128]{3,2,1,0:T(8,128)S(1)}, f32[3,2,64,128]{3,2,1,0:T(8,128)S(1)}, u32[]{:S(2)}, u32[]{:S(2)}) collective-permute-start(f32[3,2,64,128]{3,2,1,0:T(8,128)S(1)} %get-tuple-element.57), channel_id=1, source_target_pairs={{8,0},{16,8},{24,16},{32,24},{40,32},{48,40},{56,48},{64,56},{72,6... | collective-permute-start | bytes 589832 | tf_op jit(solution)/shard_map/ppermute | solution.py:18
  52.4 10.1 %copy-start.17 = (f32[8,64,128]{2,1,0:T(8,128)}, f32[8,64,128]{2,1,0:T(8,128)S(1)}, u32[]{:S(2)}) copy-start(f32[8,64,128]{2,1,0:T(8,128)S(1)} %get-tuple-element.30) | copy-start | bytes 786436
  52.4 10.1 %copy-start.19 = (f32[8,64,128]{2,1,0:T(8,128)}, f32[8,64,128]{2,1,0:T(8,128)S(1)}, u32[]{:S(2)}) copy-start(f32[8,64,128]{2,1,0:T(8,128)S(1)} %get-tuple-element.31) | copy-start | bytes 786436
  52.4 10.1 %copy-start.21 = (f32[8,64,128]{2,1,0:T(8,128)}, f32[8,64,128]{2,1,0:T(8,128)S(1)}, u32[]{:S(2)}) copy-start(f32[8,64,128]{2,1,0:T(8,128)S(1)} %get-tuple-element.33) | copy-start | bytes 786436
  52.4 10.1 %copy-start.23 = (f32[8,64,128]{2,1,0:T(8,128)}, f32[8,64,128]{2,1,0:T(8,128)S(1)}, u32[]{:S(2)}) copy-start(f32[8,64,128]{2,1,0:T(8,128)S(1)} %get-tuple-element.34) | copy-start | bytes 786436
  58.9 3.6 %copy-start.2 = (f32[10,64,128]{2,1,0:T(8,128)}, f32[10,64,128]{2,1,0:T(8,128)S(1)}, u32[]{:S(2)}) copy-start(f32[10,64,128]{2,1,0:T(8,128)S(1)} %get-tuple-element.38) | copy-start | bytes 983044
  59.3 3.8 %copy-start.5 = (f32[8,64,128]{2,1,0:T(8,128)S(1)}, f32[8,64,128]{2,1,0:T(8,128)}, u32[]{:S(2)}) copy-start(f32[8,64,128]{2,1,0:T(8,128)} %param.11) | copy-start | bytes 786436
  65.1 91.0 %reduce-scatter.5.cloned.1.call-start = ((), (), s32[]{:S(2)}) async-start(), calls=%async_computation.3 | async-start | bytes 294912 | tf_op jit(solution)/shard_map/reduce_scatter | solution.py:132
  65.2 3.8 %copy-start.3 = (f32[10,64,128]{2,1,0:T(8,128)S(1)}, f32[10,64,128]{2,1,0:T(8,128)}, u32[]{:S(2)}) copy-start(f32[10,64,128]{2,1,0:T(8,128)} %copy-done.2) | copy-start | bytes 983044
  65.2 3.8 %copy-start.6 = (f32[8,64,128]{2,1,0:T(8,128)S(1)}, f32[8,64,128]{2,1,0:T(8,128)}, u32[]{:S(2)}) copy-start(f32[8,64,128]{2,1,0:T(8,128)} %param.11) | copy-start | bytes 786436
  65.2 3.8 %copy-start.10 = (f32[8,64,128]{2,1,0:T(8,128)S(1)}, f32[8,64,128]{2,1,0:T(8,128)}, u32[]{:S(2)}) copy-start(f32[8,64,128]{2,1,0:T(8,128)} %param.10) | copy-start | bytes 786436
  65.2 3.8 %copy-start.18 = (f32[8,64,128]{2,1,0:T(8,128)S(1)}, f32[8,64,128]{2,1,0:T(8,128)}, u32[]{:S(2)}) copy-start(f32[8,64,128]{2,1,0:T(8,128)} %copy-done.17) | copy-start | bytes 786436
  65.2 3.8 %copy-start.20 = (f32[8,64,128]{2,1,0:T(8,128)S(1)}, f32[8,64,128]{2,1,0:T(8,128)}, u32[]{:S(2)}) copy-start(f32[8,64,128]{2,1,0:T(8,128)} %copy-done.19) | copy-start | bytes 786436
  65.2 3.8 %copy-start.22 = (f32[8,64,128]{2,1,0:T(8,128)S(1)}, f32[8,64,128]{2,1,0:T(8,128)}, u32[]{:S(2)}) copy-start(f32[8,64,128]{2,1,0:T(8,128)} %copy-done.21) | copy-start | bytes 786436
  65.2 3.8 %copy-start.24 = (f32[8,64,128]{2,1,0:T(8,128)S(1)}, f32[8,64,128]{2,1,0:T(8,128)}, u32[]{:S(2)}) copy-start(f32[8,64,128]{2,1,0:T(8,128)} %copy-done.23) | copy-start | bytes 786436
  65.3 3.8 %copy-start.34 = (f32[2,3,1,64,128]{4,3,2,1,0:T(8,128)S(1)}, f32[2,3,1,64,128]{4,3,2,1,0:T(8,128)}, u32[]{:S(2)}) copy-start(f32[2,3,1,64,128]{4,3,2,1,0:T(8,128)} %copy-done.33) | copy-start | bytes 589828
  70.2 2.9 %copy-start.25 = (f32[10,64,128]{2,1,0:T(8,128)S(1)}, f32[10,64,128]{2,1,0:T(8,128)}, u32[]{:S(2)}) copy-start(f32[10,64,128]{2,1,0:T(8,128)} %get-tuple-element.37) | copy-start | bytes 983044
  70.2 2.9 %copy-start.26 = (f32[10,64,128]{2,1,0:T(8,128)S(1)}, f32[10,64,128]{2,1,0:T(8,128)}, u32[]{:S(2)}) copy-start(f32[10,64,128]{2,1,0:T(8,128)} %get-tuple-element.69) | copy-start | bytes 983044
  70.2 2.9 %copy-start.27 = (f32[10,64,128]{2,1,0:T(8,128)S(1)}, f32[10,64,128]{2,1,0:T(8,128)}, u32[]{:S(2)}) copy-start(f32[10,64,128]{2,1,0:T(8,128)} %get-tuple-element.70) | copy-start | bytes 983044
  70.2 2.9 %copy-start.29 = (f32[10,64,128]{2,1,0:T(8,128)S(1)}, f32[10,64,128]{2,1,0:T(8,128)}, u32[]{:S(2)}) copy-start(f32[10,64,128]{2,1,0:T(8,128)} %get-tuple-element.67) | copy-start | bytes 983044
  (13 other events, 19.7 us)
Sparse Core Ops, SparseCore 0:
  65.2 46.5 reduce-scatter.2
  115.4 40.6 reduce-scatter.4
where the time goes:
time: 163 us
  waiting for transfers between devices  86.6 us (53%)
  starting transfers between devices  38.1 us (23%)
  between operations  14.7 us (9%)
  local copies, waits for them, and re-layouts  12 us (7%)
  other arithmetic  11.5 us (7%)
    reduce_scatter x1, waiting for transfers between devices, local(): lax.psum_scatter(bulk_total, 'event', scatter_dimension=1, tiled=True)  44.3 us
    reduce_scatter x1, waiting for transfers between devices, local(): lax.psum_scatter(shear_total, 'event', scatter_dimension=1, tiled=True)  37.2 us
    ppermute x4, starting transfers between devices, with_halo(): lax.ppermute(lax.slice_in_dim(block, 0, width, axis=dim), axis, backward)  30.2 us
    ppermute x4, starting transfers between devices, with_halo(): lax.ppermute(lax.slice_in_dim(block, block.shape[dim] - width, None, axis...  7.81 us
    slice x8, local copies, waits for them, and re-layouts, slope_mid(): upper = lax.slice_in_dim(padded, 2, padded.shape[axis], axis=axis)  7.63 us
    ppermute x4, waiting for transfers between devices, with_halo(): lax.ppermute(lax.slice_in_dim(block, 0, width, axis=dim), axis, backward)  3.77 us
  transfers between devices with their start and end apart: 10, of which 4 were waited for; matrix products, arithmetic and copies ran while one was open for 11% of the time, Pallas kernels for 0%

commit v1 on v0

v1 whole, which is shorter than its diff:
```python
import functools

import jax
import jax.numpy as jnp
from jax import lax
from jax.experimental import pallas as pl
from jax.experimental.pallas import tpu as pltpu
from jax.sharding import PartitionSpec as P

MESH = pl.DeviceIdType.MESH
time_step = 0.3
PAD = 8
ROWS = 8


def kernel(
    nb, ne, now, prev, fwd, dens, lame, mu, out, sh, bk,
    w0, w1, pv, fw, md, cf, s11, s12, s13, s22, s23, s33, part, got, res,
    lsem, hsend, hrecv, usend, urecv, rsend, rrecv, osem,
):
    layers, height = dens.shape[0], dens.shape[1]
    last = layers - 1
    band = height // ne
    me_b = lax.axis_index("blk")
    me_e = lax.axis_index("event")
    right = lax.rem(me_b + 1, nb)
    left = lax.rem(me_b + nb - 1, nb)
    body = pl.ds(PAD, height)
    chunks = range(0, height, ROWS)

    barrier = pltpu.get_barrier_semaphore()
    for b in (left, right):
        pl.semaphore_signal(barrier, inc=1, device_id={"blk": b}, device_id_type=MESH)
    for k in range(1, ne):
        pl.semaphore_signal(
            barrier, inc=1, device_id={"event": lax.rem(me_e + k, ne)}, device_id_type=MESH
        )

    own = pl.ds(1, layers)
    loc = [
        pltpu.make_async_copy(now.at[0], w0.at[:, pl.ds(2, layers), body], lsem.at[0]),
        pltpu.make_async_copy(mu, md.at[1, own], lsem.at[1]),
        pltpu.make_async_copy(lame, md.at[0, own], lsem.at[2]),
        pltpu.make_async_copy(fwd.at[0, 0], fw.at[0, :, own, body], lsem.at[3]),
        pltpu.make_async_copy(dens, cf, lsem.at[4]),
        pltpu.make_async_copy(prev.at[0], pv, lsem.at[5]),
        pltpu.make_async_copy(fwd.at[0, 1], fw.at[1, :, own, body], lsem.at[6]),
    ]
    for c in loc:
        c.start()

    blank = jnp.zeros((PAD, 128), jnp.float32)
    for top in (0, PAD + height):
        edge = pl.ds(top, PAD)
        for b in range(3):
            for i in range(1, layers + 3):
                w0[b, i, edge, :] = blank
                w1[b, i, edge, :] = blank
            for i in range(1, layers + 1):
                fw[0, b, i, edge, :] = blank
                fw[1, b, i, edge, :] = blank
        for i in range(layers):
            s12[i + 1, edge, :] = blank
            s22[i, edge, :] = blank
            s23[i, edge, :] = blank

    pl.semaphore_wait(barrier, ne + 1)

    def remote(src, dst, ss, rs, dev):
        return pltpu.make_async_remote_copy(
            src_ref=src, dst_ref=dst, send_sem=ss, recv_sem=rs, device_id=dev, device_id_type=MESH
        )

    halo = []
    for side, b in ((0, right), (1, left)):
        dev = {"blk": b}
        e2 = pl.ds(layers - 2, 2) if side == 0 else pl.ds(0, 2)
        e1 = pl.ds(last, 1) if side == 0 else pl.ds(0, 1)
        d2 = pl.ds(0, 2) if side == 0 else pl.ds(layers + 2, 2)
        d1 = pl.ds(0, 1) if side == 0 else pl.ds(layers + 1, 1)
        n = 5 * side
        halo.append([
            remote(now.at[0, :, e2], w0.at[:, d2, body], hsend.at[n], hrecv.at[n], dev),
            remote(mu.at[e1], md.at[1, d1], hsend.at[n + 1], hrecv.at[n + 1], dev),
            remote(lame.at[e1], md.at[0, d1], hsend.at[n + 2], hrecv.at[n + 2], dev),
            remote(fwd.at[0, 0, :, e1], fw.at[0, :, d1, body], hsend.at[n + 3], hrecv.at[n + 3], dev),
            remote(fwd.at[0, 1, :, e1], fw.at[1, :, d1, body], hsend.at[n + 4], hrecv.at[n + 4], dev),
        ])
    for j in range(5):
        halo[0][j].start()
        halo[1][j].start()

    lane = lax.broadcasted_iota(jnp.int32, (ROWS, 128), 1)
    first_lane = lane == 0
    last_lane = lane == 127

    def cross(c):
        return jnp.where(last_lane, 0.0, pltpu.roll(c, 127, 1)) - jnp.where(
            first_lane, 0.0, pltpu.roll(c, 1, 1)
        )

    def grads(u, i, r):
        here, up, down = pl.ds(PAD + r, ROWS), pl.ds(PAD + r + 1, ROWS), pl.ds(PAD + r - 1, ROWS)
        g1 = [u[b, i + 1, here, :] - u[b, i - 1, here, :] for b in range(3)]
        g2 = [u[b, i, up, :] - u[b, i, down, :] for b in range(3)]
        g3 = [cross(u[b, i, here, :]) for b in range(3)]
        return (
            g1[0], g2[1], g3[2], g1[1] + g2[0], g1[2] + g3[0], g2[2] + g3[1],
            g1[0] + g2[1] + g3[2],
        )

    def strain_pass(u, step, i, stress, terms):
        for r in chunks:
            rows = pl.ds(r, ROWS)
            prow = pl.ds(PAD + r, ROWS)
            a, b, c, h12, h13, h23, tr = grads(u, i + 2, r)
            if stress:
                m = md[1, i + 1, rows, :]
                lt = md[0, i + 1, rows, :] * tr
                m2 = m + m
                s11[i + 1, rows, :] = m2 * a + lt
                s12[i + 1, prow, :] = m * h12
                s13[i + 1, rows, :] = m * h13
                if stress == 2:
                    s22[i, prow, :] = m2 * b + lt
                    s23[i, prow, :] = m * h23
                    s33[i, rows, :] = m2 * c + lt
            if terms:
                fa, fb, fc, f12, f13, f23, ft = grads(fw.at[step], i + 1, r)
                bulk = tr * ft
                con = (
                    (a * fa + b * fb + c * fc)
                    + 0.5 * (h12 * f12 + h13 * f13 + h23 * f23)
                    - bulk * (1.0 / 3.0)
                )
                d, q = r // band, pl.ds(r % band, ROWS)
                if step == 0:
                    part[d, 0, i, q, :] = con
                    part[d, 1, i, q, :] = bulk
                else:
                    part[d, 0, i, q, :] += con
                    part[d, 1, i, q, :] += bulk

    def update_pass(u, former, i, store):
        for r in chunks:
            rows = pl.ds(r, ROWS)
            here, up, down = pl.ds(PAD + r, ROWS), pl.ds(PAD + r + 1, ROWS), pl.ds(PAD + r - 1, ROWS)
            k = cf[i, rows, :]
            t1 = (
                (s11[i + 2, rows, :] - s11[i, rows, :])
                + (s12[i + 1, up, :] - s12[i + 1, down, :])
                + cross(s13[i + 1, rows, :])
            )
            t2 = (
                (s12[i + 2, here, :] - s12[i, here, :])
                + (s22[i, up, :] - s22[i, down, :])
                + cross(s23[i, here, :])
            )
            t3 = (
                (s13[i + 2, rows, :] - s13[i, rows, :])
                + (s23[i, up, :] - s23[i, down, :])
                + cross(s33[i, rows, :])
            )
            for b, t in enumerate((t1, t2, t3)):
                store(b, i, r, 2.0 * u[b, i + 2, here, :] - former(b, i, r) + k * t)

    def loop(low, high, f, scale=1, offset=0):
        def step(t, carry):
            f(t * scale + offset)
            return carry

        lax.fori_loop(low, high, step, 0)

    def ends(f, low, high):
        loop(0, 2, f, high - low, low)

    for j in range(4):
        loc[j].wait()
    loop(1, last, lambda i: strain_pass(w0, 0, i, 2, True))
    loc[4].wait()
    loc[5].wait()

    def coefficient(i):
        cf[i] = (0.25 * time_step * time_step) / cf[i]

    loop(0, layers, coefficient)

    def first_former(b, i, r):
        return pv[b, i, pl.ds(r, ROWS), :]

    def first_store(b, i, r, value):
        w1[b, i + 2, pl.ds(PAD + r, ROWS), :] = value

    def first_update(i):
        update_pass(w0, first_former, i, first_store)

    loop(2, layers - 2, first_update)
    for side in (0, 1):
        for j in range(3):
            halo[side][j].wait_recv()
    ends(lambda i: strain_pass(w0, 0, i, 2, False), 0, last)
    ends(lambda i: strain_pass(w0, 0, i, 1, False), -1, layers)
    loop(layers - 2, layers, first_update)
    to_right = remote(
        w1.at[:, pl.ds(layers, 2), body], w1.at[:, pl.ds(0, 2), body],
        usend.at[0], urecv.at[0], {"blk": right},
    )
    to_right.start()
    loop(0, 2, first_update)
    to_left = remote(
        w1.at[:, pl.ds(2, 2), body], w1.at[:, pl.ds(layers + 2, 2), body],
        usend.at[1], urecv.at[1], {"blk": left},
    )
    to_left.start()
    for side in (0, 1):
        halo[side][3].wait_recv()
    ends(lambda i: strain_pass(w0, 0, i, 0, True), 0, last)

    loc[6].wait()
    loop(1, last, lambda i: strain_pass(w1, 1, i, 2, True))
    to_right.wait_recv()
    to_left.wait_recv()
    for side in (0, 1):
        halo[side][4].wait_recv()
    ends(lambda i: strain_pass(w1, 1, i, 2, True), 0, last)
    sums = []
    for k in range(1, ne):
        dest = lax.rem(me_e + k, ne)
        sums.append(remote(part.at[dest], got.at[k], rsend.at[k], rrecv.at[k], {"event": dest}))
        sums[-1].start()
    ends(lambda i: strain_pass(w1, 1, i, 1, False), -1, layers)

    def second_former(b, i, r):
        return w0[b, i + 2, pl.ds(PAD + r, ROWS), :]

    def second_store(b, i, r, value):
        res[b, i, pl.ds(r, ROWS), :] = value

    def out_copy(i):
        return pltpu.make_async_copy(res.at[:, i], out.at[0, :, i], osem.at[i])

    def second_update(i):
        update_pass(w1, second_former, i, second_store)
        out_copy(i).start()

    loop(0, layers, second_update)

    mine = pl.ds(pl.multiple_of(me_e * band, band), band)
    for k in range(ne - 1):
        sums[k].wait_recv()

    def finish(i):
        con = part[me_e, 0, i]
        bulk = part[me_e, 1, i]
        for k in range(1, ne):
            con = con + got[k, 0, i]
            bulk = bulk + got[k, 1, i]
        m = md[1, i + 1, mine, :]
        sh[i] = (-0.5 * time_step) * m * con
        bk[i] = (-0.25 * time_step) * (md[0, i + 1, mine, :] + (2.0 / 3.0) * m) * bulk

    loop(0, layers, finish)

    for i in range(layers):
        out_copy(i).wait()
    for side in (0, 1):
        for c in halo[side]:
            c.wait_send()
    to_right.wait_send()
    to_left.wait_send()
    for c in sums:
        c.wait_send()


def local(nb, ne, adjoint_now, adjoint_prev, forward_field, density, lame_first, shear_modulus):
    layers, height, width = density.shape
    tall = height + 2 * PAD
    band = height // ne
    f32 = jnp.float32
    dma = pltpu.SemaphoreType.DMA
    anywhere = pl.BlockSpec(memory_space=pl.ANY)
    vmem = pl.BlockSpec(memory_space=pltpu.VMEM)
    return pl.pallas_call(
        functools.partial(kernel, nb, ne),
        out_shape=(
            jax.ShapeDtypeStruct((1, 3, layers, height, width), f32),
            jax.ShapeDtypeStruct((layers, band, width), f32),
            jax.ShapeDtypeStruct((layers, band, width), f32),
        ),
        in_specs=[anywhere] * 6,
        out_specs=(anywhere, vmem, vmem),
        scratch_shapes=[
            pltpu.VMEM((3, layers + 4, tall, width), f32),
            pltpu.VMEM((3, layers + 4, tall, width), f32),
            pltpu.VMEM((3, layers, height, width), f32),
            pltpu.VMEM((2, 3, layers + 2, tall, width), f32),
            pltpu.VMEM((2, layers + 2, height, width), f32),
            pltpu.VMEM((layers, height, width), f32),
            pltpu.VMEM((layers + 2, height, width), f32),
            pltpu.VMEM((layers + 2, tall, width), f32),
            pltpu.VMEM((layers + 2, height, width), f32),
            pltpu.VMEM((layers, tall, width), f32),
            pltpu.VMEM((layers, tall, width), f32),
            pltpu.VMEM((layers, height, width), f32),
            pltpu.VMEM((ne, 2, layers, band, width), f32),
            pltpu.VMEM((ne, 2, layers, band, width), f32),
            pltpu.VMEM((3, layers, height, width), f32),
            dma((7,)),
            dma((10,)),
            dma((10,)),
            dma((2,)),
            dma((2,)),
            dma((ne,)),
            dma((ne,)),
            dma((layers,)),
        ],
        compiler_params=pltpu.CompilerParams(collective_id=0, has_side_effects=True),
        name="adjoint",
    )(adjoint_now, adjoint_prev, forward_field, density, lame_first, shear_modulus)


def solution(mesh):
    in_specs = (
        P("event", None, "blk", None, None),
        P("event", None, "blk", None, None),
        P("event", None, None, "blk", None, None),
        P("blk", None, None),
        P("blk", None, None),
        P("blk", None, None),
    )
    out_specs = (
        P("event", None, "blk", None, None),
        P("blk", "event", None),
        P("blk", "event", None),
    )
    body = functools.partial(local, mesh.shape["blk"], mesh.shape["event"])
    return jax.shard_map(body, mesh=mesh, in_specs=in_specs, out_specs=out_specs, check_vma=False)
```

time: 163 us -> 44.4 us (0.27)
  the two profiles are of different devices: /device:TPU:16 before, /device:TPU:14 now
where the time goes in v1:
time: 44.4 us; the launch traced here: 44.2 us
  Pallas kernels  40.2 us (91%)
  local copies, waits for them, and re-layouts  3.34 us (8%)
  between operations  0.66 us (1%)
    pallas_call x1, Pallas kernels, local(): pl.pallas_call(functools.partial(kernel, nb, ne), out_shape=(jax.ShapeDty...  40.2 us
    unnamed x7, local copies, waits for them, and re-layouts  3.34 us

profile of v1, /device:TPU:14, one launch (start us, length us, event | category | flops | bytes accessed | tf_op | source)
XLA Modules:
  0.0 44.2 jit_solution(3405575229714254269)
XLA Ops:
  0.6 40.2 %adjoint.1 = (f32[1,3,8,64,128]{4,3,2,1,0:T(8,128)}, f32[8,8,128]{2,1,0:T(8,128)}, f32[8,8,128]{2,1,0:T(8,128)}) custom-call(f32[1,3,8,64,128]{4,3,2,1,0:T(8,128)} %now.1, f32[1,3,8,64,128]{4,3,2,1,0:T(8,128)} %prev.1, f32[1,2,3,8,64,128]{5,4,3,2,1,0:T(8,128)} %fwd.1, f32[8,64,128]{2,1,0:T(8,128)} %dens.1, f32[8,64,128]{2,1,0:T(8,128)} %lame.1, f32[8,64,128]{2,1,0:T(8,128)} %mu.1), custom_call_target="tpu_custom_call" | custom-call | tf_op jit(solution)/shard_map/adjoint/pallas_call | solution.py:283
  40.9 0.0 copy-start.1
  40.9 0.0 copy-start
  40.9 2.1 %copy.12 = f32[1,3,8,64,128]{4,3,2,1,0:T(8,128)} copy(f32[1,3,8,64,128]{4,3,2,1,0:T(8,128)} %get-tuple-element.6) | data formatting | bytes 1572864
  43.0 0.0 copy-done.1
  43.0 0.6 %copy.13 = f32[8,8,128]{2,1,0:T(8,128)} copy(f32[8,8,128]{2,1,0:T(8,128)S(1)} %copy-done.1) | data formatting | bytes 65536
  43.6 0.0 copy-done
  43.6 0.6 %copy.14 = f32[8,8,128]{2,1,0:T(8,128)} copy(f32[8,8,128]{2,1,0:T(8,128)S(1)} %copy-done) | data formatting | bytes 65536
Async XLA Ops:
  40.9 2.1 %copy-start.1 = (f32[8,8,128]{2,1,0:T(8,128)S(1)}, f32[8,8,128]{2,1,0:T(8,128)}, u32[]{:S(2)}) copy-start(f32[8,8,128]{2,1,0:T(8,128)} %get-tuple-element.7) | copy-start | bytes 98308
  40.9 2.7 %copy-start = (f32[8,8,128]{2,1,0:T(8,128)S(1)}, f32[8,8,128]{2,1,0:T(8,128)}, u32[]{:S(2)}) copy-start(f32[8,8,128]{2,1,0:T(8,128)} %get-tuple-element.8) | copy-start | bytes 98308

commit v2 on v1

--- a/solution.py
+++ b/solution.py
@@ -14,9 +14,9 @@
 
 
 def kernel(
-    nb, ne, now, prev, fwd, dens, lame, mu, out, sh, bk,
-    w0, w1, pv, fw, md, cf, s11, s12, s13, s22, s23, s33, part, got, res,
-    lsem, hsend, hrecv, usend, urecv, rsend, rrecv, osem,
+    nb, ne, now, prev, fwd, dens, lame, mu, res, sh, bk,
+    w0, w1, pv, fw, md, cf, s11, s12, s13, s22, s23, s33, part, got,
+    lsem, hsend, hrecv, usend, urecv, rsend, rrecv,
 ):
     layers, height = dens.shape[0], dens.shape[1]
     last = layers - 1
@@ -46,23 +46,8 @@
         pltpu.make_async_copy(prev.at[0], pv, lsem.at[5]),
         pltpu.make_async_copy(fwd.at[0, 1], fw.at[1, :, own, body], lsem.at[6]),
     ]
-    for c in loc:
-        c.start()
-
-    blank = jnp.zeros((PAD, 128), jnp.float32)
-    for top in (0, PAD + height):
-        edge = pl.ds(top, PAD)
-        for b in range(3):
-            for i in range(1, layers + 3):
-                w0[b, i, edge, :] = blank
-                w1[b, i, edge, :] = blank
-            for i in range(1, layers + 1):
-                fw[0, b, i, edge, :] = blank
-                fw[1, b, i, edge, :] = blank
-        for i in range(layers):
-            s12[i + 1, edge, :] = blank
-            s22[i, edge, :] = blank
-            s23[i, edge, :] = blank
+    for j in range(3):
+        loc[j].start()
 
     pl.semaphore_wait(barrier, ne + 1)
 
@@ -90,6 +75,24 @@
         halo[0][j].start()
         halo[1][j].start()
 
+    for j in range(3, 7):
+        loc[j].start()
+
+    blank = jnp.zeros((PAD, 128), jnp.float32)
+    for top in (0, PAD + height):
+        edge = pl.ds(top, PAD)
+        for b in range(3):
+            for i in range(1, layers + 3):
+                w0[b, i, edge, :] = blank
+                w1[b, i, edge, :] = blank
+            for i in range(1, layers + 1):
+                fw[0, b, i, edge, :] = blank
+                fw[1, b, i, edge, :] = blank
+        for i in range(layers):
+            s12[i + 1, edge, :] = blank
+            s22[i, edge, :] = blank
+            s23[i, edge, :] = blank
+
     lane = lax.broadcasted_iota(jnp.int32, (ROWS, 128), 1)
     first_lane = lane == 0
     last_lane = lane == 127
@@ -109,7 +112,7 @@
             g1[0] + g2[1] + g3[2],
         )
 
-    def strain_pass(u, step, i, stress, terms):
+    def strain_pass(u, step, i, stress, place=None):
         for r in chunks:
             rows = pl.ds(r, ROWS)
             prow = pl.ds(PAD + r, ROWS)
@@ -125,7 +128,7 @@
                     s22[i, prow, :] = m2 * b + lt
                     s23[i, prow, :] = m * h23
                     s33[i, rows, :] = m2 * c + lt
-            if terms:
+            if place is not None:
                 fa, fb, fc, f12, f13, f23, ft = grads(fw.at[step], i + 1, r)
                 bulk = tr * ft
                 con = (
@@ -135,11 +138,11 @@
                 )
                 d, q = r // band, pl.ds(r % band, ROWS)
                 if step == 0:
-                    part[d, 0, i, q, :] = con
-                    part[d, 1, i, q, :] = bulk
+                    part[d, place, 0, q, :] = con
+                    part[d, place, 1, q, :] = bulk
                 else:
-                    part[d, 0, i, q, :] += con
-                    part[d, 1, i, q, :] += bulk
+                    part[d, place, 0, q, :] += con
+                    part[d, place, 1, q, :] += bulk
 
     def update_pass(u, former, i, store):
         for r in chunks:
@@ -164,19 +167,48 @@
             for b, t in enumerate((t1, t2, t3)):
                 store(b, i, r, 2.0 * u[b, i + 2, here, :] - former(b, i, r) + k * t)
 
-    def loop(low, high, f, scale=1, offset=0):
+    def loop(low, high, f):
         def step(t, carry):
-            f(t * scale + offset)
+            f(t)
             return carry
 
         lax.fori_loop(low, high, step, 0)
 
-    def ends(f, low, high):
-        loop(0, 2, f, high - low, low)
+    def first_former(b, i, r):
+        return pv[b, i, pl.ds(r, ROWS), :]
+
+    def first_store(b, i, r, value):
+        w1[b, i + 2, pl.ds(PAD + r, ROWS), :] = value
+
+    def first_update(i):
+        update_pass(w0, first_former, i, first_store)
+
+    def second_former(b, i, r):
+        return w0[b, i + 2, pl.ds(PAD + r, ROWS), :]
+
+    def second_store(b, i, r, value):
+        res[b, i, pl.ds(r, ROWS), :] = value
+
+    def second_update(i):
+        update_pass(w1, second_former, i, second_store)
+
+    sums = []
+
+    def send_terms(group, low, count):
+        for k in range(1, ne):
+            dest = lax.rem(me_e + k, ne)
+            n = group * ne + k
+            sums.append(remote(
+                part.at[dest, pl.ds(low, count)], got.at[k, pl.ds(low, count)],
+                rsend.at[n], rrecv.at[n], {"event": dest},
+            ))
+            sums[-1].start()
 
     for j in range(4):
         loc[j].wait()
-    loop(1, last, lambda i: strain_pass(w0, 0, i, 2, True))
+    loop(1, 3, lambda i: strain_pass(w0, 0, i, 2, i + 1))
+    loop(3, 5, lambda i: strain_pass(w0, 0, i, 2, i - 3))
+    loop(5, 7, lambda i: strain_pass(w0, 0, i, 2, i - 1))
     loc[4].wait()
     loc[5].wait()
 
@@ -184,23 +216,17 @@
         cf[i] = (0.25 * time_step * time_step) / cf[i]
 
     loop(0, layers, coefficient)
-
-    def first_former(b, i, r):
-        return pv[b, i, pl.ds(r, ROWS), :]
-
-    def first_store(b, i, r, value):
-        w1[b, i + 2, pl.ds(PAD + r, ROWS), :] = value
-
-    def first_update(i):
-        update_pass(w0, first_former, i, first_store)
-
-    loop(2, layers - 2, first_update)
+    loop(2, 6, first_update)
+    loc[6].wait()
+    loop(3, 5, lambda i: strain_pass(w1, 1, i, 2, i - 3))
+    send_terms(0, 0, 2)
+
     for side in (0, 1):
         for j in range(3):
             halo[side][j].wait_recv()
-    ends(lambda i: strain_pass(w0, 0, i, 2, False), 0, last)
-    ends(lambda i: strain_pass(w0, 0, i, 1, False), -1, layers)
-    loop(layers - 2, layers, first_update)
+    loop(0, 2, lambda t: strain_pass(w0, 0, last * t, 2))
+    loop(0, 2, lambda t: strain_pass(w0, 0, (layers + 1) * t - 1, 1))
+    loop(6, 8, first_update)
     to_right = remote(
         w1.at[:, pl.ds(layers, 2), body], w1.at[:, pl.ds(0, 2), body],
         usend.at[0], urecv.at[0], {"blk": right},
@@ -212,57 +238,38 @@
         usend.at[1], urecv.at[1], {"blk": left},
     )
     to_left.start()
+
+    loop(1, 3, lambda i: strain_pass(w1, 1, i, 2, i + 1))
+    loop(5, 7, lambda i: strain_pass(w1, 1, i, 2, i - 1))
+    send_terms(1, 2, 4)
     for side in (0, 1):
         halo[side][3].wait_recv()
-    ends(lambda i: strain_pass(w0, 0, i, 0, True), 0, last)
-
-    loc[6].wait()
-    loop(1, last, lambda i: strain_pass(w1, 1, i, 2, True))
+    loop(0, 2, lambda t: strain_pass(w0, 0, last * t, 0, 6 + t))
+    loop(2, 6, second_update)
+
     to_right.wait_recv()
     to_left.wait_recv()
     for side in (0, 1):
         halo[side][4].wait_recv()
-    ends(lambda i: strain_pass(w1, 1, i, 2, True), 0, last)
-    sums = []
-    for k in range(1, ne):
-        dest = lax.rem(me_e + k, ne)
-        sums.append(remote(part.at[dest], got.at[k], rsend.at[k], rrecv.at[k], {"event": dest}))
-        sums[-1].start()
-    ends(lambda i: strain_pass(w1, 1, i, 1, False), -1, layers)
-
-    def second_former(b, i, r):
-        return w0[b, i + 2, pl.ds(PAD + r, ROWS), :]
-
-    def second_store(b, i, r, value):
-        res[b, i, pl.ds(r, ROWS), :] = value
-
-    def out_copy(i):
-        return pltpu.make_async_copy(res.at[:, i], out.at[0, :, i], osem.at[i])
-
-    def second_update(i):
-        update_pass(w1, second_former, i, second_store)
-        out_copy(i).start()
-
-    loop(0, layers, second_update)
+    loop(0, 2, lambda t: strain_pass(w1, 1, last * t, 2, 6 + t))
+    send_terms(2, 6, 2)
+    loop(0, 2, lambda t: strain_pass(w1, 1, (layers + 1) * t - 1, 1))
+    loop(0, 2, second_update)
+    loop(6, 8, second_update)
 
     mine = pl.ds(pl.multiple_of(me_e * band, band), band)
-    for k in range(ne - 1):
-        sums[k].wait_recv()
-
-    def finish(i):
-        con = part[me_e, 0, i]
-        bulk = part[me_e, 1, i]
+    for c in sums:
+        c.wait_recv()
+    for p, i in enumerate((3, 4, 1, 2, 5, 6, 0, 7)):
+        con = part[me_e, p, 0]
+        bulk = part[me_e, p, 1]
         for k in range(1, ne):
-            con = con + got[k, 0, i]
-            bulk = bulk + got[k, 1, i]
+            con = con + got[k, p, 0]
+            bulk = bulk + got[k, p, 1]
         m = md[1, i + 1, mine, :]
         sh[i] = (-0.5 * time_step) * m * con
         bk[i] = (-0.25 * time_step) * (md[0, i + 1, mine, :] + (2.0 / 3.0) * m) * bulk
 
-    loop(0, layers, finish)
-
-    for i in range(layers):
-        out_copy(i).wait()
     for side in (0, 1):
         for c in halo[side]:
             c.wait_send()
@@ -270,6 +277,18 @@
     to_left.wait_send()
     for c in sums:
         c.wait_send()
+
+
+def put_out(field, shear, bulk, field_out, shear_out, bulk_out, sem):
+    copies = [
+        pltpu.make_async_copy(field, field_out.at[0], sem.at[0]),
+        pltpu.make_async_copy(shear, shear_out, sem.at[1]),
+        pltpu.make_async_copy(bulk, bulk_out, sem.at[2]),
+    ]
+    for c in copies:
+        c.start()
+    for c in copies:
+        c.wait()
 
 
 def local(nb, ne, adjoint_now, adjoint_prev, forward_field, density, lame_first, shear_modulus):
@@ -280,15 +299,15 @@
     dma = pltpu.SemaphoreType.DMA
     anywhere = pl.BlockSpec(memory_space=pl.ANY)
     vmem = pl.BlockSpec(memory_space=pltpu.VMEM)
-    return pl.pallas_call(
+    results = pl.pallas_call(
         functools.partial(kernel, nb, ne),
         out_shape=(
-            jax.ShapeDtypeStruct((1, 3, layers, height, width), f32),
-            jax.ShapeDtypeStruct((layers, band, width), f32),
-            jax.ShapeDtypeStruct((layers, band, width), f32),
+            pltpu.VMEM((3, layers, height, width), f32),
+            pltpu.VMEM((layers, band, width), f32),
+            pltpu.VMEM((layers, band, width), f32),
         ),
         in_specs=[anywhere] * 6,
-        out_specs=(anywhere, vmem, vmem),
+        out_specs=(vmem,) * 3,
         scratch_shapes=[
             pltpu.VMEM((3, layers + 4, tall, width), f32),
             pltpu.VMEM((3, layers + 4, tall, width), f32),
@@ -302,21 +321,32 @@
             pltpu.VMEM((layers, tall, width), f32),
             pltpu.VMEM((layers, tall, width), f32),
             pltpu.VMEM((layers, height, width), f32),
-            pltpu.VMEM((ne, 2, layers, band, width), f32),
-            pltpu.VMEM((ne, 2, layers, band, width), f32),
-            pltpu.VMEM((3, layers, height, width), f32),
+            pltpu.VMEM((ne, layers, 2, band, width), f32),
+            pltpu.VMEM((ne, layers, 2, band, width), f32),
             dma((7,)),
             dma((10,)),
             dma((10,)),
             dma((2,)),
             dma((2,)),
-            dma((ne,)),
-            dma((ne,)),
-            dma((layers,)),
+            dma((3 * ne,)),
+            dma((3 * ne,)),
         ],
         compiler_params=pltpu.CompilerParams(collective_id=0, has_side_effects=True),
         name="adjoint",
     )(adjoint_now, adjoint_prev, forward_field, density, lame_first, shear_modulus)
+    return pl.pallas_call(
+        put_out,
+        out_shape=(
+            jax.ShapeDtypeStruct((1, 3, layers, height, width), f32),
+            jax.ShapeDtypeStruct((layers, band, width), f32),
+            jax.ShapeDtypeStruct((layers, band, width), f32),
+        ),
+        in_specs=[anywhere] * 3,
+        out_specs=(anywhere,) * 3,
+        scratch_shapes=[dma((3,))],
+        compiler_params=pltpu.CompilerParams(vmem_limit_bytes=1 << 20),
+        name="put_out",
+    )(*results)
 
 
 def solution(mesh):

time: 44.4 us -> 42.8 us (0.964)
  the two profiles are of different devices: /device:TPU:14 before, /device:TPU:2 now
where the time goes in v2:
time: 42.8 us; the launch traced here: 42.7 us
  Pallas kernels  42.1 us (98%)
  between operations  0.64 us (1%)
    pallas_call x1, Pallas kernels, local(): pl.pallas_call(functools.partial(kernel, nb, ne), out_shape=(pltpu.VMEM((...  41.1 us
    pallas_call x1, Pallas kernels, local(): pl.pallas_call(put_out, out_shape=(jax.ShapeDtypeStruct((1, 3, layers, he...  0.91 us

profile of v2, /device:TPU:2, one launch (start us, length us, event | category | flops | bytes accessed | tf_op | source)
XLA Modules:
  0.0 42.7 jit_solution(8463403754307087598)
XLA Ops:
  0.6 41.1 %adjoint.1 = (f32[3,8,64,128]{3,2,1,0:T(8,128)S(1)}, f32[8,8,128]{2,1,0:T(8,128)S(1)}, f32[8,8,128]{2,1,0:T(8,128)S(1)}) custom-call(f32[1,3,8,64,128]{4,3,2,1,0:T(8,128)} %now.1, f32[1,3,8,64,128]{4,3,2,1,0:T(8,128)} %prev.1, f32[1,2,3,8,64,128]{5,4,3,2,1,0:T(8,128)} %fwd.1, f32[8,64,128]{2,1,0:T(8,128)} %dens.1, f32[8,64,128]{2,1,0:T(8,128)} %lame.1, ...), custom_call_target="tpu_custom_call" | custom-call | tf_op jit(solution)/shard_map/adjoint/pallas_call | solution.py:302
  41.8 0.9 %put_out.1 = (f32[1,3,8,64,128]{4,3,2,1,0:T(8,128)}, f32[8,8,128]{2,1,0:T(8,128)}, f32[8,8,128]{2,1,0:T(8,128)}) custom-call(f32[3,8,64,128]{3,2,1,0:T(8,128)S(1)} %get-tuple-element.6.field, f32[8,8,128]{2,1,0:T(8,128)S(1)} %get-tuple-element.7.shear, f32[8,8,128]{2,1,0:T(8,128)S(1)} %get-tuple-element.8.bulk), custom_call_target="tpu_custom_call" | custom-call | tf_op jit(solution)/shard_map/put_out/pallas_call | solution.py:337

commit v3 on v2

--- a/solution.py
+++ b/solution.py
@@ -14,9 +14,9 @@
 
 
 def kernel(
-    nb, ne, now, prev, fwd, dens, lame, mu, res, sh, bk,
-    w0, w1, pv, fw, md, cf, s11, s12, s13, s22, s23, s33, part, got,
-    lsem, hsend, hrecv, usend, urecv, rsend, rrecv,
+    nb, ne, run, now, prev, fwd, dens, lame, mu, res, sh, bk,
+    w0, w1, pv, fw, md, cf, s11, s12, s13, s22, s23, s33, part, got, passed,
+    lsem, hsend, hrecv, usend, urecv, rsend, rrecv, psend, precv, fsend,
 ):
     layers, height = dens.shape[0], dens.shape[1]
     last = layers - 1
@@ -26,10 +26,18 @@
     right = lax.rem(me_b + 1, nb)
     left = lax.rem(me_b + nb - 1, nb)
     body = pl.ds(PAD, height)
+
+    spot = lax.rem(me_b, run)
+    is_head = spot == 0
+    is_tail = spot == run - 1
+    at_edge = jnp.logical_or(is_head, is_tail)
+    tail = lax.div(spot, run - 1)
+    mirror = me_b - spot + (run - 1 - spot)
+    beyond = lax.rem(me_b + run * (1 - 2 * tail) + nb, nb)
     chunks = range(0, height, ROWS)
 
     barrier = pltpu.get_barrier_semaphore()
-    for b in (left, right):
+    for b in (left, right, mirror, lax.rem(me_b + run, nb), lax.rem(me_b + nb - run, nb)):
         pl.semaphore_signal(barrier, inc=1, device_id={"blk": b}, device_id_type=MESH)
     for k in range(1, ne):
         pl.semaphore_signal(
@@ -49,7 +57,7 @@
     for j in range(3):
         loc[j].start()
 
-    pl.semaphore_wait(barrier, ne + 1)
+    pl.semaphore_wait(barrier, ne + 4)
 
     def remote(src, dst, ss, rs, dev):
         return pltpu.make_async_remote_copy(
@@ -71,9 +79,37 @@
             remote(fwd.at[0, 0, :, e1], fw.at[0, :, d1, body], hsend.at[n + 3], hrecv.at[n + 3], dev),
             remote(fwd.at[0, 1, :, e1], fw.at[1, :, d1, body], hsend.at[n + 4], hrecv.at[n + 4], dev),
         ])
-    for j in range(5):
+    for j in range(3):
         halo[0][j].start()
         halo[1][j].start()
+    edge_layer = pl.ds(last * tail, 1)
+    handed = [
+        remote(fwd.at[0, j, :, edge_layer], passed.at[j], psend.at[j], precv.at[j], {"blk": mirror})
+        for j in range(2)
+    ]
+    far_layer = pl.ds((layers + 1) * tail, 1)
+    onward = [
+        remote(
+            passed.at[j], fw.at[j, :, far_layer, body], fsend.at[j], hrecv.at[5 * tail + 3 + j],
+            {"blk": beyond},
+        )
+        for j in range(2)
+    ]
+
+    @pl.when(at_edge)
+    def _():
+        for c in handed:
+            c.start()
+
+    @pl.when(jnp.logical_not(is_tail))
+    def _():
+        halo[0][3].start()
+        halo[0][4].start()
+
+    @pl.when(jnp.logical_not(is_head))
+    def _():
+        halo[1][3].start()
+        halo[1][4].start()
 
     for j in range(3, 7):
         loc[j].start()
@@ -217,6 +253,13 @@
 
     loop(0, layers, coefficient)
     loop(2, 6, first_update)
+
+    @pl.when(at_edge)
+    def _():
+        for j in range(2):
+            handed[j].wait_recv()
+            onward[j].start()
+
     loc[6].wait()
     loop(3, 5, lambda i: strain_pass(w1, 1, i, 2, i - 3))
     send_terms(0, 0, 2)
@@ -227,17 +270,19 @@
     loop(0, 2, lambda t: strain_pass(w0, 0, last * t, 2))
     loop(0, 2, lambda t: strain_pass(w0, 0, (layers + 1) * t - 1, 1))
     loop(6, 8, first_update)
-    to_right = remote(
-        w1.at[:, pl.ds(layers, 2), body], w1.at[:, pl.ds(0, 2), body],
-        usend.at[0], urecv.at[0], {"blk": right},
-    )
-    to_right.start()
+    def edge_copy(source, target, n, b):
+        return remote(
+            w1.at[:, pl.ds(source, 1), body], w1.at[:, pl.ds(target, 1), body],
+            usend.at[n], urecv.at[n], {"blk": b},
+        )
+
+    near = [edge_copy(layers + 1, 1, 0, right), edge_copy(2, layers + 2, 1, left)]
+    far = [edge_copy(layers, 0, 2, right), edge_copy(3, layers + 3, 3, left)]
+    near[0].start()
+    far[0].start()
     loop(0, 2, first_update)
-    to_left = remote(
-        w1.at[:, pl.ds(2, 2), body], w1.at[:, pl.ds(layers + 2, 2), body],
-        usend.at[1], urecv.at[1], {"blk": left},
-    )
-    to_left.start()
+    near[1].start()
+    far[1].start()
 
     loop(1, 3, lambda i: strain_pass(w1, 1, i, 2, i + 1))
     loop(5, 7, lambda i: strain_pass(w1, 1, i, 2, i - 1))
@@ -247,12 +292,14 @@
     loop(0, 2, lambda t: strain_pass(w0, 0, last * t, 0, 6 + t))
     loop(2, 6, second_update)
 
-    to_right.wait_recv()
-    to_left.wait_recv()
+    for c in near:
+        c.wait_recv()
     for side in (0, 1):
         halo[side][4].wait_recv()
     loop(0, 2, lambda t: strain_pass(w1, 1, last * t, 2, 6 + t))
     send_terms(2, 6, 2)
+    for c in far:
+        c.wait_recv()
     loop(0, 2, lambda t: strain_pass(w1, 1, (layers + 1) * t - 1, 1))
     loop(0, 2, second_update)
     loop(6, 8, second_update)
@@ -271,10 +318,26 @@
         bk[i] = (-0.25 * time_step) * (md[0, i + 1, mine, :] + (2.0 / 3.0) * m) * bulk
 
     for side in (0, 1):
-        for c in halo[side]:
+        for c in halo[side][:3]:
             c.wait_send()
-    to_right.wait_send()
-    to_left.wait_send()
+
+    @pl.when(at_edge)
+    def _():
+        for c in handed + onward:
+            c.wait_send()
+
+    @pl.when(jnp.logical_not(is_tail))
+    def _():
+        halo[0][3].wait_send()
+        halo[0][4].wait_send()
+
+    @pl.when(jnp.logical_not(is_head))
+    def _():
+        halo[1][3].wait_send()
+        halo[1][4].wait_send()
+
+    for c in near + far:
+        c.wait_send()
     for c in sums:
         c.wait_send()
 
@@ -295,12 +358,13 @@
     layers, height, width = density.shape
     tall = height + 2 * PAD
     band = height // ne
+    run = 16 if nb % 16 == 0 else 2
     f32 = jnp.float32
     dma = pltpu.SemaphoreType.DMA
     anywhere = pl.BlockSpec(memory_space=pl.ANY)
     vmem = pl.BlockSpec(memory_space=pltpu.VMEM)
     results = pl.pallas_call(
-        functools.partial(kernel, nb, ne),
+        functools.partial(kernel, nb, ne, run),
         out_shape=(
             pltpu.VMEM((3, layers, height, width), f32),
             pltpu.VMEM((layers, band, width), f32),
@@ -323,13 +387,17 @@
             pltpu.VMEM((layers, height, width), f32),
             pltpu.VMEM((ne, layers, 2, band, width), f32),
             pltpu.VMEM((ne, layers, 2, band, width), f32),
+            pltpu.VMEM((2, 3, 1, height, width), f32),
             dma((7,)),
             dma((10,)),
             dma((10,)),
+            dma((4,)),
+            dma((4,)),
+            dma((3 * ne,)),
+            dma((3 * ne,)),
             dma((2,)),
             dma((2,)),
-            dma((3 * ne,)),
-            dma((3 * ne,)),
+            dma((2,)),
         ],
         compiler_params=pltpu.CompilerParams(collective_id=0, has_side_effects=True),
         name="adjoint",

time: 42.8 us -> 38.2 us (0.89)
  Pallas kernels: 42.1 us -> 37.4 us
    pallas_call x1, Pallas kernels: 41.1 us -> 36.5 us  [local(): pl.pallas_call(functools.partial(kernel, nb, ne, run), out_shape=(pltpu.V...]
where the time goes in v3:
time: 38.2 us; the launch traced here: 38.1 us
  Pallas kernels  37.4 us (98%)
  between operations  0.64 us (2%)
    pallas_call x1, Pallas kernels, local(): pl.pallas_call(functools.partial(kernel, nb, ne, run), out_shape=(pltpu.V...  36.5 us
    pallas_call x1, Pallas kernels, local(): pl.pallas_call(put_out, out_shape=(jax.ShapeDtypeStruct((1, 3, layers, he...  0.91 us

profile of v3, /device:TPU:2, one launch (start us, length us, event | category | flops | bytes accessed | tf_op | source)
XLA Modules:
  0.0 38.1 jit_solution(17336999106008418483)
XLA Ops:
  0.6 36.5 %adjoint.1 = (f32[3,8,64,128]{3,2,1,0:T(8,128)S(1)}, f32[8,8,128]{2,1,0:T(8,128)S(1)}, f32[8,8,128]{2,1,0:T(8,128)S(1)}) custom-call(f32[1,3,8,64,128]{4,3,2,1,0:T(8,128)} %now.1, f32[1,3,8,64,128]{4,3,2,1,0:T(8,128)} %prev.1, f32[1,2,3,8,64,128]{5,4,3,2,1,0:T(8,128)} %fwd.1, f32[8,64,128]{2,1,0:T(8,128)} %dens.1, f32[8,64,128]{2,1,0:T(8,128)} %lame.1, ...), custom_call_target="tpu_custom_call" | custom-call | tf_op jit(solution)/shard_map/adjoint/pallas_call | solution.py:366
  37.2 0.9 %put_out.1 = (f32[1,3,8,64,128]{4,3,2,1,0:T(8,128)}, f32[8,8,128]{2,1,0:T(8,128)}, f32[8,8,128]{2,1,0:T(8,128)}) custom-call(f32[3,8,64,128]{3,2,1,0:T(8,128)S(1)} %get-tuple-element.6.field, f32[8,8,128]{2,1,0:T(8,128)S(1)} %get-tuple-element.7.shear, f32[8,8,128]{2,1,0:T(8,128)S(1)} %get-tuple-element.8.bulk), custom_call_target="tpu_custom_call" | custom-call | tf_op jit(solution)/shard_map/put_out/pallas_call | solution.py:405

commit v4 on v3

--- a/solution.py
+++ b/solution.py
@@ -15,7 +15,7 @@
 
 def kernel(
     nb, ne, run, now, prev, fwd, dens, lame, mu, res, sh, bk,
-    w0, w1, pv, fw, md, cf, s11, s12, s13, s22, s23, s33, part, got, passed,
+    w0, w1, pv, fw, md, cf, s11, s12, s13, s22, s23, s33, part, got, passed, passed_now,
     lsem, hsend, hrecv, usend, urecv, rsend, rrecv, psend, precv, fsend,
 ):
     layers, height = dens.shape[0], dens.shape[1]
@@ -67,31 +67,44 @@
     halo = []
     for side, b in ((0, right), (1, left)):
         dev = {"blk": b}
-        e2 = pl.ds(layers - 2, 2) if side == 0 else pl.ds(0, 2)
+        e2 = pl.ds(last - 1, 1) if side == 0 else pl.ds(1, 1)
         e1 = pl.ds(last, 1) if side == 0 else pl.ds(0, 1)
-        d2 = pl.ds(0, 2) if side == 0 else pl.ds(layers + 2, 2)
+        d3 = pl.ds(0, 1) if side == 0 else pl.ds(layers + 3, 1)
+        d2 = pl.ds(1, 1) if side == 0 else pl.ds(layers + 2, 1)
         d1 = pl.ds(0, 1) if side == 0 else pl.ds(layers + 1, 1)
-        n = 5 * side
+        n = 6 * side
         halo.append([
-            remote(now.at[0, :, e2], w0.at[:, d2, body], hsend.at[n], hrecv.at[n], dev),
+            remote(now.at[0, :, e1], w0.at[:, d2, body], hsend.at[n], hrecv.at[n], dev),
             remote(mu.at[e1], md.at[1, d1], hsend.at[n + 1], hrecv.at[n + 1], dev),
             remote(lame.at[e1], md.at[0, d1], hsend.at[n + 2], hrecv.at[n + 2], dev),
-            remote(fwd.at[0, 0, :, e1], fw.at[0, :, d1, body], hsend.at[n + 3], hrecv.at[n + 3], dev),
-            remote(fwd.at[0, 1, :, e1], fw.at[1, :, d1, body], hsend.at[n + 4], hrecv.at[n + 4], dev),
+            remote(now.at[0, :, e2], w0.at[:, d3, body], hsend.at[n + 3], hrecv.at[n + 3], dev),
+            remote(fwd.at[0, 0, :, e1], fw.at[0, :, d1, body], hsend.at[n + 4], hrecv.at[n + 4], dev),
+            remote(fwd.at[0, 1, :, e1], fw.at[1, :, d1, body], hsend.at[n + 5], hrecv.at[n + 5], dev),
         ])
     for j in range(3):
         halo[0][j].start()
         halo[1][j].start()
     edge_layer = pl.ds(last * tail, 1)
+    inner_layer = pl.ds(1 + (last - 2) * tail, 1)
     handed = [
-        remote(fwd.at[0, j, :, edge_layer], passed.at[j], psend.at[j], precv.at[j], {"blk": mirror})
+        remote(now.at[0, :, inner_layer], passed_now, psend.at[0], precv.at[0], {"blk": mirror})
+    ] + [
+        remote(
+            fwd.at[0, j, :, edge_layer], passed.at[j], psend.at[j + 1], precv.at[j + 1],
+            {"blk": mirror},
+        )
         for j in range(2)
     ]
     far_layer = pl.ds((layers + 1) * tail, 1)
     onward = [
         remote(
-            passed.at[j], fw.at[j, :, far_layer, body], fsend.at[j], hrecv.at[5 * tail + 3 + j],
-            {"blk": beyond},
+            passed_now, w0.at[:, pl.ds((layers + 3) * tail, 1), body],
+            fsend.at[0], hrecv.at[6 * tail + 3], {"blk": beyond},
+        )
+    ] + [
+        remote(
+            passed.at[j], fw.at[j, :, far_layer, body], fsend.at[j + 1],
+            hrecv.at[6 * tail + 4 + j], {"blk": beyond},
         )
         for j in range(2)
     ]
@@ -103,13 +116,13 @@
 
     @pl.when(jnp.logical_not(is_tail))
     def _():
-        halo[0][3].start()
-        halo[0][4].start()
+        for c in halo[0][3:]:
+            c.start()
 
     @pl.when(jnp.logical_not(is_head))
     def _():
-        halo[1][3].start()
-        halo[1][4].start()
+        for c in halo[1][3:]:
+            c.start()
 
     for j in range(3, 7):
         loc[j].start()
@@ -243,6 +256,12 @@
     for j in range(4):
         loc[j].wait()
     loop(1, 3, lambda i: strain_pass(w0, 0, i, 2, i + 1))
+
+    @pl.when(at_edge)
+    def _():
+        handed[0].wait_recv()
+        onward[0].start()
+
     loop(3, 5, lambda i: strain_pass(w0, 0, i, 2, i - 3))
     loop(5, 7, lambda i: strain_pass(w0, 0, i, 2, i - 1))
     loc[4].wait()
@@ -256,7 +275,7 @@
 
     @pl.when(at_edge)
     def _():
-        for j in range(2):
+        for j in (1, 2):
             handed[j].wait_recv()
             onward[j].start()
 
@@ -265,11 +284,10 @@
     send_terms(0, 0, 2)
 
     for side in (0, 1):
-        for j in range(3):
+        for j in range(4):
             halo[side][j].wait_recv()
     loop(0, 2, lambda t: strain_pass(w0, 0, last * t, 2))
     loop(0, 2, lambda t: strain_pass(w0, 0, (layers + 1) * t - 1, 1))
-    loop(6, 8, first_update)
     def edge_copy(source, target, n, b):
         return remote(
             w1.at[:, pl.ds(source, 1), body], w1.at[:, pl.ds(target, 1), body],
@@ -278,24 +296,26 @@
 
     near = [edge_copy(layers + 1, 1, 0, right), edge_copy(2, layers + 2, 1, left)]
     far = [edge_copy(layers, 0, 2, right), edge_copy(3, layers + 3, 3, left)]
+    loop(7, 8, first_update)
     near[0].start()
+    loop(0, 1, first_update)
+    near[1].start()
+    loop(0, 2, lambda t: first_update(1 + 5 * t))
     far[0].start()
-    loop(0, 2, first_update)
-    near[1].start()
     far[1].start()
 
     loop(1, 3, lambda i: strain_pass(w1, 1, i, 2, i + 1))
     loop(5, 7, lambda i: strain_pass(w1, 1, i, 2, i - 1))
     send_terms(1, 2, 4)
     for side in (0, 1):
-        halo[side][3].wait_recv()
+        halo[side][4].wait_recv()
     loop(0, 2, lambda t: strain_pass(w0, 0, last * t, 0, 6 + t))
     loop(2, 6, second_update)
 
     for c in near:
         c.wait_recv()
     for side in (0, 1):
-        halo[side][4].wait_recv()
+        halo[side][5].wait_recv()
     loop(0, 2, lambda t: strain_pass(w1, 1, last * t, 2, 6 + t))
     send_terms(2, 6, 2)
     for c in far:
@@ -328,13 +348,13 @@
 
     @pl.when(jnp.logical_not(is_tail))
     def _():
-        halo[0][3].wait_send()
-        halo[0][4].wait_send()
+        for c in halo[0][3:]:
+            c.wait_send()
 
     @pl.when(jnp.logical_not(is_head))
     def _():
-        halo[1][3].wait_send()
-        halo[1][4].wait_send()
+        for c in halo[1][3:]:
+            c.wait_send()
 
     for c in near + far:
         c.wait_send()
@@ -388,16 +408,17 @@
             pltpu.VMEM((ne, layers, 2, band, width), f32),
             pltpu.VMEM((ne, layers, 2, band, width), f32),
             pltpu.VMEM((2, 3, 1, height, width), f32),
+            pltpu.VMEM((3, 1, height, width), f32),
             dma((7,)),
-            dma((10,)),
-            dma((10,)),
+            dma((12,)),
+            dma((12,)),
             dma((4,)),
             dma((4,)),
             dma((3 * ne,)),
             dma((3 * ne,)),
-            dma((2,)),
-            dma((2,)),
-            dma((2,)),
+            dma((3,)),
+            dma((3,)),
+            dma((3,)),
         ],
         compiler_params=pltpu.CompilerParams(collective_id=0, has_side_effects=True),
         name="adjoint",

time: 38.2 us -> 38.1 us (level)
  no operation moved by 1% of the time
where the time goes in v4:
time: 38.1 us; the launch traced here: 37.9 us
  Pallas kernels  37.3 us (98%)
  between operations  0.64 us (2%)
    pallas_call x1, Pallas kernels, local(): pl.pallas_call(functools.partial(kernel, nb, ne, run), out_shape=(pltpu.V...  36.4 us
    pallas_call x1, Pallas kernels, local(): pl.pallas_call(put_out, out_shape=(jax.ShapeDtypeStruct((1, 3, layers, he...  0.91 us

profile of v4, /device:TPU:2, one launch (start us, length us, event | category | flops | bytes accessed | tf_op | source)
XLA Modules:
  0.0 37.9 jit_solution(8305232480203214785)
XLA Ops:
  0.6 36.4 %adjoint.1 = (f32[3,8,64,128]{3,2,1,0:T(8,128)S(1)}, f32[8,8,128]{2,1,0:T(8,128)S(1)}, f32[8,8,128]{2,1,0:T(8,128)S(1)}) custom-call(f32[1,3,8,64,128]{4,3,2,1,0:T(8,128)} %now.1, f32[1,3,8,64,128]{4,3,2,1,0:T(8,128)} %prev.1, f32[1,2,3,8,64,128]{5,4,3,2,1,0:T(8,128)} %fwd.1, f32[8,64,128]{2,1,0:T(8,128)} %dens.1, f32[8,64,128]{2,1,0:T(8,128)} %lame.1, ...), custom_call_target="tpu_custom_call" | custom-call | tf_op jit(solution)/shard_map/adjoint/pallas_call | solution.py:386
  37.0 0.9 %put_out.1 = (f32[1,3,8,64,128]{4,3,2,1,0:T(8,128)}, f32[8,8,128]{2,1,0:T(8,128)}, f32[8,8,128]{2,1,0:T(8,128)}) custom-call(f32[3,8,64,128]{3,2,1,0:T(8,128)S(1)} %get-tuple-element.6.field, f32[8,8,128]{2,1,0:T(8,128)S(1)} %get-tuple-element.7.shear, f32[8,8,128]{2,1,0:T(8,128)S(1)} %get-tuple-element.8.bulk), custom_call_target="tpu_custom_call" | custom-call | tf_op jit(solution)/shard_map/put_out/pallas_call | solution.py:426

commit v5 on v4

--- a/solution.py
+++ b/solution.py
@@ -283,43 +283,86 @@
     loop(3, 5, lambda i: strain_pass(w1, 1, i, 2, i - 3))
     send_terms(0, 0, 2)
 
-    for side in (0, 1):
-        for j in range(4):
-            halo[side][j].wait_recv()
-    loop(0, 2, lambda t: strain_pass(w0, 0, last * t, 2))
-    loop(0, 2, lambda t: strain_pass(w0, 0, (layers + 1) * t - 1, 1))
+    early = is_head.astype(jnp.int32)
+
+    def face(n):
+        return early + n * (1 - 2 * early)
+
+    def arrival(side, j):
+        d1 = pl.ds((layers + 1) * side, 1)
+        sem = hrecv.at[6 * side + j]
+        if j == 0:
+            dst = w0.at[:, pl.ds(1 + (layers + 1) * side, 1), body]
+        elif j == 3:
+            dst = w0.at[:, pl.ds((layers + 3) * side, 1), body]
+        elif j in (1, 2):
+            dst = md.at[2 - j, d1]
+        else:
+            dst = fw.at[j - 4, :, d1, body]
+        return remote(dst, dst, hsend.at[6 * side + j], sem, {"blk": left})
+
     def edge_copy(source, target, n, b):
         return remote(
             w1.at[:, pl.ds(source, 1), body], w1.at[:, pl.ds(target, 1), body],
             usend.at[n], urecv.at[n], {"blk": b},
         )
 
-    near = [edge_copy(layers + 1, 1, 0, right), edge_copy(2, layers + 2, 1, left)]
-    far = [edge_copy(layers, 0, 2, right), edge_copy(3, layers + 3, 3, left)]
-    loop(7, 8, first_update)
-    near[0].start()
-    loop(0, 1, first_update)
-    near[1].start()
-    loop(0, 2, lambda t: first_update(1 + 5 * t))
-    far[0].start()
-    far[1].start()
+    def edge_copies(side):
+        b = lax.rem(me_b + nb + 2 * side - 1, nb)
+        there = 1 - side
+        return (
+            edge_copy(2 + last * side, 1 + (layers + 1) * there, there, b),
+            edge_copy(3 + (last - 2) * side, (layers + 3) * there, 2 + there, b),
+        )
+
+    def first_edge(n):
+        side = face(n)
+        for j in range(4):
+            arrival(side, j).wait_recv()
+        strain_pass(w0, 0, last * side, 2)
+        strain_pass(w0, 0, (layers + 1) * side - 1, 1)
+        near, far = edge_copies(side)
+        first_update(last * side)
+        near.start()
+        first_update(1 + (last - 2) * side)
+        far.start()
+
+    loop(0, 2, first_edge)
 
     loop(1, 3, lambda i: strain_pass(w1, 1, i, 2, i + 1))
     loop(5, 7, lambda i: strain_pass(w1, 1, i, 2, i - 1))
     send_terms(1, 2, 4)
+    loop(2, 6, second_update)
+
+    def forward_edge(n):
+        side = face(n)
+        arrival(side, 4).wait_recv()
+        strain_pass(w0, 0, last * side, 0, 6 + side)
+
+    loop(0, 2, forward_edge)
+
+    def terms_copy(side, k):
+        dest = lax.rem(me_e + k, ne)
+        m = (2 + side) * ne + k
+        return remote(
+            part.at[dest, pl.ds(6 + side, 1)], got.at[k, pl.ds(6 + side, 1)],
+            rsend.at[m], rrecv.at[m], {"event": dest},
+        )
+
+    def second_edge(n):
+        side = face(n)
+        edge_copy(2, 1 + (layers + 1) * side, side, left).wait_recv()
+        arrival(side, 5).wait_recv()
+        strain_pass(w1, 1, last * side, 2, 6 + side)
+        for k in range(1, ne):
+            terms_copy(side, k).start()
+
+    loop(0, 2, second_edge)
     for side in (0, 1):
-        halo[side][4].wait_recv()
-    loop(0, 2, lambda t: strain_pass(w0, 0, last * t, 0, 6 + t))
-    loop(2, 6, second_update)
-
-    for c in near:
-        c.wait_recv()
+        for k in range(1, ne):
+            sums.append(terms_copy(side, k))
     for side in (0, 1):
-        halo[side][5].wait_recv()
-    loop(0, 2, lambda t: strain_pass(w1, 1, last * t, 2, 6 + t))
-    send_terms(2, 6, 2)
-    for c in far:
-        c.wait_recv()
+        edge_copy(2, (layers + 3) * side, 2 + side, left).wait_recv()
     loop(0, 2, lambda t: strain_pass(w1, 1, (layers + 1) * t - 1, 1))
     loop(0, 2, second_update)
     loop(6, 8, second_update)
@@ -356,8 +399,9 @@
         for c in halo[1][3:]:
             c.wait_send()
 
-    for c in near + far:
-        c.wait_send()
+    for side in (0, 1):
+        for c in edge_copies(side):
+            c.wait_send()
     for c in sums:
         c.wait_send()
 
@@ -414,8 +458,8 @@
             dma((12,)),
             dma((4,)),
             dma((4,)),
-            dma((3 * ne,)),
-            dma((3 * ne,)),
+            dma((4 * ne,)),
+            dma((4 * ne,)),
             dma((3,)),
             dma((3,)),
             dma((3,)),

time: 38.1 us -> 37.5 us (0.984)
  the two profiles are of different devices: /device:TPU:2 before, /device:TPU:8 now
where the time goes in v5:
time: 37.5 us; the launch traced here: 37.4 us
  Pallas kernels  36.7 us (98%)
  between operations  0.64 us (2%)
    pallas_call x1, Pallas kernels, local(): pl.pallas_call(functools.partial(kernel, nb, ne, run), out_shape=(pltpu.V...  35.8 us
    pallas_call x1, Pallas kernels, local(): pl.pallas_call(put_out, out_shape=(jax.ShapeDtypeStruct((1, 3, layers, he...  0.91 us

profile of v5, /device:TPU:8, one launch (start us, length us, event | category | flops | bytes accessed | tf_op | source)
XLA Modules:
  0.0 37.4 jit_solution(12785807111446522809)
XLA Ops:
  0.6 35.8 %adjoint.1 = (f32[3,8,64,128]{3,2,1,0:T(8,128)S(1)}, f32[8,8,128]{2,1,0:T(8,128)S(1)}, f32[8,8,128]{2,1,0:T(8,128)S(1)}) custom-call(f32[1,3,8,64,128]{4,3,2,1,0:T(8,128)} %now.1, f32[1,3,8,64,128]{4,3,2,1,0:T(8,128)} %prev.1, f32[1,2,3,8,64,128]{5,4,3,2,1,0:T(8,128)} %fwd.1, f32[8,64,128]{2,1,0:T(8,128)} %dens.1, f32[8,64,128]{2,1,0:T(8,128)} %lame.1, ...), custom_call_target="tpu_custom_call" | custom-call | tf_op jit(solution)/shard_map/adjoint/pallas_call | solution.py:430
  36.5 0.9 %put_out.1 = (f32[1,3,8,64,128]{4,3,2,1,0:T(8,128)}, f32[8,8,128]{2,1,0:T(8,128)}, f32[8,8,128]{2,1,0:T(8,128)}) custom-call(f32[3,8,64,128]{3,2,1,0:T(8,128)S(1)} %get-tuple-element.6.field, f32[8,8,128]{2,1,0:T(8,128)S(1)} %get-tuple-element.7.shear, f32[8,8,128]{2,1,0:T(8,128)S(1)} %get-tuple-element.8.bulk), custom_call_target="tpu_custom_call" | custom-call | tf_op jit(solution)/shard_map/put_out/pallas_call | solution.py:470

commit v6 on v5

--- a/solution.py
+++ b/solution.py
@@ -368,9 +368,14 @@
     loop(6, 8, second_update)
 
     mine = pl.ds(pl.multiple_of(me_e * band, band), band)
-    for c in sums:
-        c.wait_recv()
+    inside = 2 * (ne - 1)
     for p, i in enumerate((3, 4, 1, 2, 5, 6, 0, 7)):
+        if p == 0:
+            for c in sums[:inside]:
+                c.wait_recv()
+        if p == 6:
+            for c in sums[inside:]:
+                c.wait_recv()
         con = part[me_e, p, 0]
         bulk = part[me_e, p, 1]
         for k in range(1, ne):

time: 37.5 us -> 37.5 us (level)
  no operation moved by 1% of the time
where the time goes in v6:
time: 37.5 us; the launch traced here: 37.4 us
  Pallas kernels  36.7 us (98%)
  between operations  0.64 us (2%)
    pallas_call x1, Pallas kernels, local(): pl.pallas_call(functools.partial(kernel, nb, ne, run), out_shape=(pltpu.V...  35.8 us
    pallas_call x1, Pallas kernels, local(): pl.pallas_call(put_out, out_shape=(jax.ShapeDtypeStruct((1, 3, layers, he...  0.91 us

profile of v6, /device:TPU:8, one launch (start us, length us, event | category | flops | bytes accessed | tf_op | source)
XLA Modules:
  0.0 37.4 jit_solution(5391633038459244522)
XLA Ops:
  0.6 35.8 %adjoint.1 = (f32[3,8,64,128]{3,2,1,0:T(8,128)S(1)}, f32[8,8,128]{2,1,0:T(8,128)S(1)}, f32[8,8,128]{2,1,0:T(8,128)S(1)}) custom-call(f32[1,3,8,64,128]{4,3,2,1,0:T(8,128)} %now.1, f32[1,3,8,64,128]{4,3,2,1,0:T(8,128)} %prev.1, f32[1,2,3,8,64,128]{5,4,3,2,1,0:T(8,128)} %fwd.1, f32[8,64,128]{2,1,0:T(8,128)} %dens.1, f32[8,64,128]{2,1,0:T(8,128)} %lame.1, ...), custom_call_target="tpu_custom_call" | custom-call | tf_op jit(solution)/shard_map/adjoint/pallas_call | solution.py:435
  36.5 0.9 %put_out.1 = (f32[1,3,8,64,128]{4,3,2,1,0:T(8,128)}, f32[8,8,128]{2,1,0:T(8,128)}, f32[8,8,128]{2,1,0:T(8,128)}) custom-call(f32[3,8,64,128]{3,2,1,0:T(8,128)S(1)} %get-tuple-element.6.field, f32[8,8,128]{2,1,0:T(8,128)S(1)} %get-tuple-element.7.shear, f32[8,8,128]{2,1,0:T(8,128)S(1)} %get-tuple-element.8.bulk), custom_call_target="tpu_custom_call" | custom-call | tf_op jit(solution)/shard_map/put_out/pallas_call | solution.py:475
